TPU v7x, 32 devices: a whole 2x2x4 slice. The times are simulated.
32 devices in a mesh: comp: 4 (over y, core), dom: 8 (over z, x).
Axes of the slice: x: 2, y: 2, z: 4, core: 2. Of those that a mesh axis runs over, the one named last changes fastest.
Arguments:
- source_field: bfloat16 [4, 8, 32, 16, 128], P('comp', 'dom'), may hold values from -108 to 108, as said below
- source_block: int32 [4, 8, 12], P('comp', 'dom'), may hold values from 0 to 31
- margin: int32 [4, 8, 12, 2], P('comp', 'dom'), may hold values from 0 to 31, as said below
- remap_weight: bfloat16 [4, 8, 12, 128, 128], P('comp', 'dom'), may hold values from 0 to 0.7, as said below
- helm_coef: float32 [256, 512], P('dom', 'comp'), may hold values from 0.05 to 1
Outputs:
- solution: float32 [16, 256, 512], P(None, 'dom', 'comp')
- residual: float32 [16, 256, 512], P(None, 'dom', 'comp')
Inputs may be any that keep to these rules, and one draw needn't show every extreme that they name: `source_field`: each value is a normal or uniform draw times scales that vary by field level, cell and device. `margin`: for each device and each owner, at most 4 of the device's entries name that owner and they name at most 2 distinct target rows; on every device some owner has exactly 4 entries. `remap_weight`: Nonnegative.
All inputs are finite; a program needn't handle non-finite values.
Results may differ from a plain program's by a relative error of at most 0.0003.
Values sent between devices are 32-bit elements; how exact they have to be, the bound alone decides.
No kernel may reach another device: no remote copies, remote signals or barrier semaphores. Data moves between devices by JAX's collectives and lax.ppermute only.
A program may use at most 64 MiB of HBM per device.

v0:
```python
import jax
import jax.numpy as jnp
from jax import lax
from jax.sharding import PartitionSpec as P

CAP = 4
ITERS = 2
HIGHEST = lax.Precision.HIGHEST


def with_halo(array, sides, width):
    for axis, dim in sides:
        devices, length = (lax.axis_size(axis), array.shape[dim])
        up = [(i, (i + 1) % devices) for i in range(devices - 1)]
        down = [(j, i) for i, j in up]
        last = lax.slice_in_dim(array, length - width, length, axis=dim)
        initial = lax.slice_in_dim(array, 0, width, axis=dim)
        before = lax.ppermute(last, axis, up)
        after = lax.ppermute(initial, axis, down)
        array = jnp.concatenate([before, array, after], axis=dim)
    return array


def row_dots(left, right):
    return jnp.sum(left * right, axis=(1, 2))


def operate(current, helm_coef):
    padded = with_halo(current, (("comp", 2), ("dom", 1)), 1)
    beside = padded[:, 2:, 1:-1] + padded[:, :-2, 1:-1] + padded[:, 1:-1, 2:] + padded[:, 1:-1, :-2]
    return (4.0 + helm_coef) * current - beside


def two_products(residual, applied):
    return lax.psum((row_dots(residual, residual), row_dots(residual, applied)), ("comp", "dom"))


def per_device(source_field, source_block, margin, remap_weight, helm_coef):
    sources = source_field[0, 0]
    block_ids = source_block[0, 0]
    peer_ids = margin[0, 0, :, 0]
    row_dest = margin[0, 0, :, 1]
    weights = remap_weight[0, 0]
    picked = jnp.take(sources, block_ids, axis=0)
    remapped = jnp.einsum("krs,kts->krt", picked, weights, preferred_element_type=jnp.float32)
    groups = lax.axis_size("comp")
    entries = peer_ids.shape[0]
    rows_here = helm_coef.shape[0]
    position = jnp.arange(entries, dtype=jnp.int32)
    earlier = position[None, :] < position[:, None]
    same_peer = peer_ids[:, None] == peer_ids[None, :]
    slot_ids = jnp.sum(earlier & same_peer, axis=1)
    slot_width = CAP
    slot_total = groups * slot_width
    placing = (
        (peer_ids * slot_width + slot_ids)[:, None]
        == jnp.arange(slot_total, dtype=jnp.int32)[None, :]
    ).astype(jnp.float32)
    outgoing = jnp.einsum("ks,krb->srb", placing, remapped, precision=HIGHEST)
    labels = jnp.max(placing * (row_dest + 1).astype(jnp.float32)[:, None], axis=0) - 1.0
    arrived, arrived_labels = (
        lax.all_to_all(outgoing, "comp", split_axis=0, concat_axis=0, tiled=True),
        lax.all_to_all(labels, "comp", split_axis=0, concat_axis=0, tiled=True),
    )
    landing = (
        arrived_labels.astype(jnp.int32)[:, None] == jnp.arange(rows_here, dtype=jnp.int32)[None, :]
    ).astype(jnp.float32)
    target = jnp.einsum("st,srb->rtb", landing, arrived, precision=HIGHEST)
    solution = jnp.zeros_like(target)
    residual = target
    applied = operate(residual, helm_coef)
    norm_now, product = two_products(residual, applied)
    step_len = norm_now / product
    direction = residual
    along = applied
    for step in range(ITERS):
        solution = solution + step_len[:, None, None] * direction
        residual = residual - step_len[:, None, None] * along
        if step + 1 < ITERS:
            applied = operate(residual, helm_coef)
            norm_next, product = two_products(residual, applied)
            ratio = norm_next / norm_now
            step_len = norm_next / (product - ratio * norm_next / step_len)
            direction = residual + ratio[:, None, None] * direction
            along = applied + ratio[:, None, None] * along
            norm_now = norm_next
    return (solution, residual)


def solution(mesh):
    placed = (
        P("comp", "dom", None, None, None),
        P("comp", "dom", None),
        P("comp", "dom", None, None),
        P("comp", "dom", None, None, None),
        P("dom", "comp"),
    )
    return jax.shard_map(
        per_device,
        mesh=mesh,
        in_specs=placed,
        out_specs=(P(None, "dom", "comp"), P(None, "dom", "comp")),
        check_vma=False,
    )
```

profile of v0, /device:TPU:0, one launch (start us, length us, event | category | flops | bytes accessed | tf_op | source)
XLA Modules:
  0.0 140.9 jit_solution(12832660203048157975)
XLA Ops:
  0.6 0.0 copy-start
  0.6 0.8 convert_bitcast_fusion
  1.4 0.0 copy-start.2
  1.4 0.2 convert_reduce_fusion
  1.6 0.5 copy-done.2
  2.1 0.1 select_reduce_fusion
  2.2 0.7 sub.21
  2.9 0.0 copy-start.3
  2.9 4.4 %all-to-all-start.1 = ((f32[4,4,1]{1,2,0:T(1,128)}), f32[4,4,1]{1,2,0:T(1,128)S(1)}, u32[]{:S(2)}, u32[]{:S(2)}) async-start(f32[4,4,1]{1,2,0:T(1,128)} %bitcast.8), calls=%async_computation.1 | async-start | bytes 4096 | tf_op jit(solution)/shard_map/all_to_all | solution.py:63
  7.2 0.0 copy-done.3
  7.3 1.5 %gather_fusion = bf16[12,16,128]{2,1,0:T(8,128)(2,1)S(1)} fusion(bf16[32,16,128]{2,1,0:T(8,128)(2,1)} %bitcast.25, s32[1024]{0:T(1024)S(1)} %pad_clamp_fusion), kind=kCustom, calls=%fused_computation | custom fusion | bytes 98352 | tf_op jit(solution)/shard_map/jit(_take)/gather | solution.py:44
  8.8 0.0 copy-done
  8.8 0.3 fusion
  9.1 0.3 fusion.11
  9.5 0.7 copy.11
  10.2 0.8 all-to-all-done.1
  11.0 3.3 %all-to-all-start = ((f32[16,16,128]{2,1,0:T(8,128)}), f32[16,16,128]{2,1,0:T(8,128)S(1)}, u32[]{:S(2)}, u32[]{:S(2)}) async-start(f32[16,16,128]{2,1,0:T(8,128)} %copy.11), calls=%async_computation | async-start | bytes 262144 | tf_op jit(solution)/shard_map/all_to_all | solution.py:62
  14.3 0.1 convert_element_type.29
  14.4 4.5 %all-to-all-done = f32[16,16,128]{2,1,0:T(8,128)S(1)} async-done(((f32[16,16,128]{2,1,0:T(8,128)}), f32[16,16,128]{2,1,0:T(8,128)S(1)}, u32[]{:S(2)}, u32[]{:S(2)}) %all-to-all-start) | async-done | bytes 131104 | tf_op jit(solution)/shard_map/all_to_all | solution.py:62
  18.9 0.4 convolution_bitcast_fusion
  19.2 0.1 fusion.27
  19.4 1.3 collective-permute-start.1
  20.7 0.0 copy-start.1
  20.7 3.0 %collective-permute-start = (f32[16,32,1]{2,1,0:T(8,128)S(1)}, f32[16,32,1]{2,1,0:T(8,128)S(1)}, u32[]{:S(2)}, u32[]{:S(2)}) collective-permute-start(f32[16,32,1]{2,1,0:T(8,128)S(1)} %get-tuple-element.22), channel_id=1, source_target_pairs={{0,8},{8,16},{16,24},{1,9},{9,17},{17,25},{2,10},{10,18},{18,26},{... | collective-permute-start | bytes 6152 | tf_op jit(solution)/shard_map/ppermute | solution.py:18
  23.8 0.0 collective-permute-done.1
  23.8 1.1 collective-permute-done
  24.9 0.2 pad_maximum_fusion.21
  25.1 1.3 collective-permute-start.2
  26.4 4.5 %collective-permute-start.3 = (f32[16,1,130]{2,1,0:T(1,128)S(1)}, f32[16,1,130]{2,1,0:T(1,128)S(1)}, u32[]{:S(2)}, u32[]{:S(2)}) collective-permute-start(f32[16,1,130]{2,1,0:T(1,128)S(1)} %get-tuple-element.16), channel_id=1, source_target_pairs={{0,1},{1,2},{2,3},{3,4},{4,5},{5,6},{6,7},{8,9},{9,10},{10,11},{11... | collective-permute-start | bytes 24968 | tf_op jit(solution)/shard_map/ppermute | solution.py:18
  30.9 0.0 copy-done.1
  30.9 0.0 collective-permute-done.2
  30.9 1.4 collective-permute-done.3
  32.3 0.8 multiply_reduce_fusion.2
  33.1 45.7 %all-reduce.1 = (f32[16]{0:T(128)S(1)}, f32[16]{0:T(128)S(1)}) all-reduce(f32[16]{0:T(128)S(1)} %get-tuple-element.5, f32[16]{0:T(128)S(1)} %get-tuple-element.4), channel_id=1, replica_groups=mesh['comp'=4,'dom'=8] {'comp','dom'}, use_global_device_ids=true, to_apply=%region_3.4 | all-reduce | flops 32 | bytes 256 | tf_op jit(solution)/shard_map/psum | solution.py:35
  78.8 0.1 multiply_subtract_fusion.1
  78.9 0.1 fusion.26
  79.1 1.3 collective-permute-start.5
  80.4 3.0 %collective-permute-start.4 = (f32[16,32,1]{2,1,0:T(8,128)S(1)}, f32[16,32,1]{2,1,0:T(8,128)S(1)}, u32[]{:S(2)}, u32[]{:S(2)}) collective-permute-start(f32[16,32,1]{2,1,0:T(8,128)S(1)} %get-tuple-element.20), channel_id=1, source_target_pairs={{0,8},{8,16},{16,24},{1,9},{9,17},{17,25},{2,10},{10,18},{18,26},{... | collective-permute-start | bytes 6152 | tf_op jit(solution)/shard_map/ppermute | solution.py:18
  83.4 0.0 collective-permute-done.5
  83.4 1.1 collective-permute-done.4
  84.5 0.2 pad_maximum_fusion.18
  84.7 1.3 collective-permute-start.6
  86.0 4.8 %collective-permute-start.7 = (f32[16,1,130]{2,1,0:T(1,128)S(1)}, f32[16,1,130]{2,1,0:T(1,128)S(1)}, u32[]{:S(2)}, u32[]{:S(2)}) collective-permute-start(f32[16,1,130]{2,1,0:T(1,128)S(1)} %get-tuple-element.14), channel_id=1, source_target_pairs={{0,1},{1,2},{2,3},{3,4},{4,5},{5,6},{6,7},{8,9},{9,10},{10,11},{11... | collective-permute-start | bytes 24968 | tf_op jit(solution)/shard_map/ppermute | solution.py:18
  90.8 0.0 collective-permute-done.6
  90.8 1.4 %collective-permute-done.7 = f32[16,1,130]{2,1,0:T(1,128)S(1)} collective-permute-done((f32[16,1,130]{2,1,0:T(1,128)S(1)}, f32[16,1,130]{2,1,0:T(1,128)S(1)}, u32[]{:S(2)}, u32[]{:S(2)}) %collective-permute-start.7) | collective-permute-done | bytes 8352 | tf_op jit(solution)/shard_map/ppermute | solution.py:18
  92.3 0.8 multiply_reduce_fusion
  93.0 46.6 %all-reduce = (f32[16]{0:T(128)S(1)}, f32[16]{0:T(128)S(1)}) all-reduce(f32[16]{0:T(128)S(1)} %get-tuple-element.3, f32[16]{0:T(128)S(1)} %get-tuple-element.2), channel_id=1, replica_groups=mesh['comp'=4,'dom'=8] {'comp','dom'}, use_global_device_ids=true, to_apply=%region_7.8 | all-reduce | flops 32 | bytes 256 | tf_op jit(solution)/shard_map/psum | solution.py:35
  139.6 1.2 multiply_subtract_fusion
  (9 shorter events, 0.1 us)
Async XLA Ops:
  0.6 8.1 %copy-start = (bf16[1,1,12,128,128]{4,3,2,1,0:T(8,128)(2,1)S(1)}, bf16[1,1,12,128,128]{4,3,2,1,0:T(8,128)(2,1)}, u32[]{:S(2)}) copy-start(bf16[1,1,12,128,128]{4,3,2,1,0:T(8,128)(2,1)} %param.8) | copy-start | bytes 1179652
  1.4 0.7 copy-start.2
  2.9 4.4 %copy-start.3 = (s32[1,1,12]{2,1,0:T(1,128)S(1)}, s32[1,1,12]{2,1,0:T(1,128)}, u32[]{:S(2)}) copy-start(s32[1,1,12]{2,1,0:T(1,128)} %param.6) | copy-start | bytes 148
  2.9 8.1 %all-to-all-start.1 = ((f32[4,4,1]{1,2,0:T(1,128)}), f32[4,4,1]{1,2,0:T(1,128)S(1)}, u32[]{:S(2)}, u32[]{:S(2)}) async-start(f32[4,4,1]{1,2,0:T(1,128)} %bitcast.8), calls=%async_computation.1 | async-start | bytes 4096 | tf_op jit(solution)/shard_map/all_to_all | solution.py:63
  11.0 7.9 %all-to-all-start = ((f32[16,16,128]{2,1,0:T(8,128)}), f32[16,16,128]{2,1,0:T(8,128)S(1)}, u32[]{:S(2)}, u32[]{:S(2)}) async-start(f32[16,16,128]{2,1,0:T(8,128)} %copy.11), calls=%async_computation | async-start | bytes 262144 | tf_op jit(solution)/shard_map/all_to_all | solution.py:62
  19.4 4.4 %collective-permute-start.1 = (f32[16,32,1]{2,1,0:T(8,128)S(1)}, f32[16,32,1]{2,1,0:T(8,128)S(1)}, u32[]{:S(2)}, u32[]{:S(2)}) collective-permute-start(f32[16,32,1]{2,1,0:T(8,128)S(1)} %get-tuple-element.21), channel_id=1, source_target_pairs={{8,0},{16,8},{24,16},{9,1},{17,9},{25,17},{10,2},{18,10},{26,18},{... | collective-permute-start | bytes 6152 | tf_op jit(solution)/shard_map/ppermute | solution.py:19
  20.7 10.2 %copy-start.1 = (f32[32,128]{1,0:T(8,128)S(1)}, f32[32,128]{1,0:T(8,128)}, u32[]{:S(2)}) copy-start(f32[32,128]{1,0:T(8,128)} %param.9) | copy-start | bytes 49156
  20.7 4.2 %collective-permute-start = (f32[16,32,1]{2,1,0:T(8,128)S(1)}, f32[16,32,1]{2,1,0:T(8,128)S(1)}, u32[]{:S(2)}, u32[]{:S(2)}) collective-permute-start(f32[16,32,1]{2,1,0:T(8,128)S(1)} %get-tuple-element.22), channel_id=1, source_target_pairs={{0,8},{8,16},{16,24},{1,9},{9,17},{17,25},{2,10},{10,18},{18,26},{... | collective-permute-start | bytes 6152 | tf_op jit(solution)/shard_map/ppermute | solution.py:18
  25.1 5.9 %collective-permute-start.2 = (f32[16,1,130]{2,1,0:T(1,128)S(1)}, f32[16,1,130]{2,1,0:T(1,128)S(1)}, u32[]{:S(2)}, u32[]{:S(2)}) collective-permute-start(f32[16,1,130]{2,1,0:T(1,128)S(1)} %get-tuple-element.15), channel_id=1, source_target_pairs={{1,0},{2,1},{3,2},{4,3},{5,4},{6,5},{7,6},{9,8},{10,9},{11,10},{12... | collective-permute-start | bytes 24968 | tf_op jit(solution)/shard_map/ppermute | solution.py:19
  26.4 6.0 %collective-permute-start.3 = (f32[16,1,130]{2,1,0:T(1,128)S(1)}, f32[16,1,130]{2,1,0:T(1,128)S(1)}, u32[]{:S(2)}, u32[]{:S(2)}) collective-permute-start(f32[16,1,130]{2,1,0:T(1,128)S(1)} %get-tuple-element.16), channel_id=1, source_target_pairs={{0,1},{1,2},{2,3},{3,4},{4,5},{5,6},{6,7},{8,9},{9,10},{10,11},{11... | collective-permute-start | bytes 24968 | tf_op jit(solution)/shard_map/ppermute | solution.py:18
  79.1 4.4 %collective-permute-start.5 = (f32[16,32,1]{2,1,0:T(8,128)S(1)}, f32[16,32,1]{2,1,0:T(8,128)S(1)}, u32[]{:S(2)}, u32[]{:S(2)}) collective-permute-start(f32[16,32,1]{2,1,0:T(8,128)S(1)} %get-tuple-element.19), channel_id=1, source_target_pairs={{8,0},{16,8},{24,16},{9,1},{17,9},{25,17},{10,2},{18,10},{26,18},{... | collective-permute-start | bytes 6152 | tf_op jit(solution)/shard_map/ppermute | solution.py:19
  80.4 4.2 %collective-permute-start.4 = (f32[16,32,1]{2,1,0:T(8,128)S(1)}, f32[16,32,1]{2,1,0:T(8,128)S(1)}, u32[]{:S(2)}, u32[]{:S(2)}) collective-permute-start(f32[16,32,1]{2,1,0:T(8,128)S(1)} %get-tuple-element.20), channel_id=1, source_target_pairs={{0,8},{8,16},{16,24},{1,9},{9,17},{17,25},{2,10},{10,18},{18,26},{... | collective-permute-start | bytes 6152 | tf_op jit(solution)/shard_map/ppermute | solution.py:18
  84.7 6.1 %collective-permute-start.6 = (f32[16,1,130]{2,1,0:T(1,128)S(1)}, f32[16,1,130]{2,1,0:T(1,128)S(1)}, u32[]{:S(2)}, u32[]{:S(2)}) collective-permute-start(f32[16,1,130]{2,1,0:T(1,128)S(1)} %get-tuple-element.13), channel_id=1, source_target_pairs={{1,0},{2,1},{3,2},{4,3},{5,4},{6,5},{7,6},{9,8},{10,9},{11,10},{12... | collective-permute-start | bytes 24968 | tf_op jit(solution)/shard_map/ppermute | solution.py:19
  86.0 6.2 %collective-permute-start.7 = (f32[16,1,130]{2,1,0:T(1,128)S(1)}, f32[16,1,130]{2,1,0:T(1,128)S(1)}, u32[]{:S(2)}, u32[]{:S(2)}) collective-permute-start(f32[16,1,130]{2,1,0:T(1,128)S(1)} %get-tuple-element.14), channel_id=1, source_target_pairs={{0,1},{1,2},{2,3},{3,4},{4,5},{5,6},{6,7},{8,9},{9,10},{10,11},{11... | collective-permute-start | bytes 24968 | tf_op jit(solution)/shard_map/ppermute | solution.py:18
where the time goes:
time: 141 us
  blocking collectives  92.3 us (65%)
  starting transfers between devices  28.3 us (20%)
  waiting for transfers between devices  10.3 us (7%)
  other arithmetic  4.26 us (3%)
  local copies, waits for them, and re-layouts  3.7 us (3%)
    psum x2, blocking collectives, two_products(): lax.psum((row_dots(residual, residual), row_dots(residual, applied)), ('c...  92.3 us
    ppermute x4, starting transfers between devices, with_halo(): before = lax.ppermute(last, axis, up)  15.4 us
    ppermute x4, starting transfers between devices, with_halo(): after = lax.ppermute(initial, axis, down)  5.17 us
    ppermute x4, waiting for transfers between devices, with_halo(): before = lax.ppermute(last, axis, up)  5.04 us
    all_to_all x1, waiting for transfers between devices, per_device(): lax.all_to_all(outgoing, 'comp', split_axis=0, concat_axis=0, tiled=True)  4.46 us
    all_to_all x1, starting transfers between devices, per_device(): lax.all_to_all(labels, 'comp', split_axis=0, concat_axis=0, tiled=True)  4.4 us
    all_to_all x1, starting transfers between devices, per_device(): lax.all_to_all(outgoing, 'comp', split_axis=0, concat_axis=0, tiled=True)  3.33 us
  transfers between devices with their start and end apart: 10, of which 6 were waited for; matrix products, arithmetic and copies ran while one was open for 2% of the time, Pallas kernels for 0%

commit v1 on v0

--- a/solution.py
+++ b/solution.py
@@ -32,7 +32,13 @@
 
 
 def two_products(residual, applied):
-    return lax.psum((row_dots(residual, residual), row_dots(residual, applied)), ("comp", "dom"))
+
+    def render_units_here(v0):
+        for t in ("dom", "comp"):
+            v0 = lax.psum(v0, t)
+        return v0
+
+    return render_units_here((row_dots(residual, residual), row_dots(residual, applied)))
 
 
 def per_device(source_field, source_block, margin, remap_weight, helm_coef):

time: 141 us -> 110 us (0.78)
  blocking collectives: 92.3 us -> 60.9 us
    psum x2 -> x4, blocking collectives: 92.3 us -> 60.9 us  [render_units_here(): v0 = lax.psum(v0, t)]
  transfers between devices with their start and end apart: 10 -> 10, of which waited for: 6 -> 6; matrix products, arithmetic and copies ran while one was open for 2% -> 3% of each run, Pallas kernels for 0% -> 0%
where the time goes in v1:
time: 110 us; the launch traced here: 109 us
  blocking collectives  60.9 us (55%)
  starting transfers between devices  28.1 us (26%)
  waiting for transfers between devices  10.3 us (9%)
  other arithmetic  4.27 us (4%)
  local copies, waits for them, and re-layouts  3.7 us (3%)
    psum x4, blocking collectives, render_units_here(): v0 = lax.psum(v0, t)  60.9 us
    ppermute x4, starting transfers between devices, with_halo(): before = lax.ppermute(last, axis, up)  15.2 us
    ppermute x4, starting transfers between devices, with_halo(): after = lax.ppermute(initial, axis, down)  5.17 us
    ppermute x4, waiting for transfers between devices, with_halo(): before = lax.ppermute(last, axis, up)  5.04 us
    all_to_all x1, waiting for transfers between devices, per_device(): lax.all_to_all(outgoing, 'comp', split_axis=0, concat_axis=0, tiled=True)  4.46 us
    all_to_all x1, starting transfers between devices, per_device(): lax.all_to_all(labels, 'comp', split_axis=0, concat_axis=0, tiled=True)  4.4 us
    all_to_all x1, starting transfers between devices, per_device(): lax.all_to_all(outgoing, 'comp', split_axis=0, concat_axis=0, tiled=True)  3.33 us
  transfers between devices with their start and end apart: 10, of which 6 were waited for; matrix products, arithmetic and copies ran while one was open for 3% of the time, Pallas kernels for 0%

profile of v1, /device:TPU:0, one launch (start us, length us, event | category | flops | bytes accessed | tf_op | source)
XLA Modules:
  0.0 109.2 jit_solution(13379285308597822890)
XLA Ops:
  0.6 0.0 copy-start
  0.6 0.8 convert_bitcast_fusion
  1.4 0.2 convert_reduce_fusion
  1.6 0.5 copy-done.2
  2.1 0.1 select_reduce_fusion
  2.2 0.7 sub.21
  2.9 4.4 %all-to-all-start.1 = ((f32[4,4,1]{1,2,0:T(1,128)}), f32[4,4,1]{1,2,0:T(1,128)S(1)}, u32[]{:S(2)}, u32[]{:S(2)}) async-start(f32[4,4,1]{1,2,0:T(1,128)} %bitcast.8), calls=%async_computation.1 | async-start | bytes 4096 | tf_op jit(solution)/shard_map/all_to_all | solution.py:69
  7.2 0.0 copy-done.3
  7.3 1.5 %gather_fusion = bf16[12,16,128]{2,1,0:T(8,128)(2,1)S(1)} fusion(bf16[32,16,128]{2,1,0:T(8,128)(2,1)} %bitcast.25, s32[1024]{0:T(1024)S(1)} %pad_clamp_fusion), kind=kCustom, calls=%fused_computation | custom fusion | bytes 98352 | tf_op jit(solution)/shard_map/jit(_take)/gather | solution.py:50
  8.8 0.0 copy-done
  8.8 0.3 fusion
  9.1 0.3 fusion.11
  9.5 0.7 copy.11
  10.2 0.8 all-to-all-done.1
  11.0 3.3 %all-to-all-start = ((f32[16,16,128]{2,1,0:T(8,128)}), f32[16,16,128]{2,1,0:T(8,128)S(1)}, u32[]{:S(2)}, u32[]{:S(2)}) async-start(f32[16,16,128]{2,1,0:T(8,128)} %copy.11), calls=%async_computation | async-start | bytes 262144 | tf_op jit(solution)/shard_map/all_to_all | solution.py:68
  14.3 0.1 convert_element_type.29
  14.4 4.5 %all-to-all-done = f32[16,16,128]{2,1,0:T(8,128)S(1)} async-done(((f32[16,16,128]{2,1,0:T(8,128)}), f32[16,16,128]{2,1,0:T(8,128)S(1)}, u32[]{:S(2)}, u32[]{:S(2)}) %all-to-all-start) | async-done | bytes 131104 | tf_op jit(solution)/shard_map/all_to_all | solution.py:68
  18.9 0.4 convolution_bitcast_fusion
  19.2 0.1 fusion.27
  19.4 1.3 %collective-permute-start.1 = (f32[16,32,1]{2,1,0:T(8,128)S(1)}, f32[16,32,1]{2,1,0:T(8,128)S(1)}, u32[]{:S(2)}, u32[]{:S(2)}) collective-permute-start(f32[16,32,1]{2,1,0:T(8,128)S(1)} %get-tuple-element.25), channel_id=1, source_target_pairs={{8,0},{16,8},{24,16},{9,1},{17,9},{25,17},{10,2},{18,10},{26,18},{... | collective-permute-start | bytes 6152 | tf_op jit(solution)/shard_map/ppermute | solution.py:19
  20.7 0.0 copy-start.1
  20.7 3.0 %collective-permute-start = (f32[16,32,1]{2,1,0:T(8,128)S(1)}, f32[16,32,1]{2,1,0:T(8,128)S(1)}, u32[]{:S(2)}, u32[]{:S(2)}) collective-permute-start(f32[16,32,1]{2,1,0:T(8,128)S(1)} %get-tuple-element.26), channel_id=1, source_target_pairs={{0,8},{8,16},{16,24},{1,9},{9,17},{17,25},{2,10},{10,18},{18,26},{... | collective-permute-start | bytes 6152 | tf_op jit(solution)/shard_map/ppermute | solution.py:18
  23.8 0.0 collective-permute-done.1
  23.8 1.1 %collective-permute-done = f32[16,32,1]{2,1,0:T(8,128)S(1)} collective-permute-done((f32[16,32,1]{2,1,0:T(8,128)S(1)}, f32[16,32,1]{2,1,0:T(8,128)S(1)}, u32[]{:S(2)}, u32[]{:S(2)}) %collective-permute-start) | collective-permute-done | bytes 2080 | tf_op jit(solution)/shard_map/ppermute | solution.py:18
  24.9 0.2 pad_maximum_fusion.21
  25.1 1.3 %collective-permute-start.2 = (f32[16,1,130]{2,1,0:T(1,128)S(1)}, f32[16,1,130]{2,1,0:T(1,128)S(1)}, u32[]{:S(2)}, u32[]{:S(2)}) collective-permute-start(f32[16,1,130]{2,1,0:T(1,128)S(1)} %get-tuple-element.19), channel_id=1, source_target_pairs={{1,0},{2,1},{3,2},{4,3},{5,4},{6,5},{7,6},{9,8},{10,9},{11,10},{12... | collective-permute-start | bytes 24968 | tf_op jit(solution)/shard_map/ppermute | solution.py:19
  26.4 4.5 %collective-permute-start.3 = (f32[16,1,130]{2,1,0:T(1,128)S(1)}, f32[16,1,130]{2,1,0:T(1,128)S(1)}, u32[]{:S(2)}, u32[]{:S(2)}) collective-permute-start(f32[16,1,130]{2,1,0:T(1,128)S(1)} %get-tuple-element.20), channel_id=1, source_target_pairs={{0,1},{1,2},{2,3},{3,4},{4,5},{5,6},{6,7},{8,9},{9,10},{10,11},{11... | collective-permute-start | bytes 24968 | tf_op jit(solution)/shard_map/ppermute | solution.py:18
  30.9 0.0 copy-done.1
  30.9 0.0 collective-permute-done.2
  30.9 1.4 %collective-permute-done.3 = f32[16,1,130]{2,1,0:T(1,128)S(1)} collective-permute-done((f32[16,1,130]{2,1,0:T(1,128)S(1)}, f32[16,1,130]{2,1,0:T(1,128)S(1)}, u32[]{:S(2)}, u32[]{:S(2)}) %collective-permute-start.3) | collective-permute-done | bytes 8352 | tf_op jit(solution)/shard_map/ppermute | solution.py:18
  32.3 0.8 multiply_reduce_fusion.2
  33.1 22.8 %all-reduce.1 = (f32[16]{0:T(128)S(1)}, f32[16]{0:T(128)S(1)}) all-reduce(f32[16]{0:T(128)S(1)} %get-tuple-element.5, f32[16]{0:T(128)S(1)} %get-tuple-element.4), channel_id=1, replica_groups=mesh['comp'=4,'dom'=8] {'dom'}, use_global_device_ids=true, to_apply=%region_3.4 | all-reduce | flops 32 | bytes 256 | tf_op jit(solution)/shard_map/psum | solution.py:38
  55.9 8.8 %all-reduce.3 = (f32[16]{0:T(128)S(1)}, f32[16]{0:T(128)S(1)}) all-reduce(f32[16]{0:T(128)S(1)} %get-tuple-element.8, f32[16]{0:T(128)S(1)} %get-tuple-element.9), channel_id=1, replica_groups=mesh['comp'=4,'dom'=8] {'comp'}, use_global_device_ids=true, to_apply=%region_4.5 | all-reduce | flops 32 | bytes 256 | tf_op jit(solution)/shard_map/psum | solution.py:38
  64.7 0.1 multiply_subtract_fusion.1
  64.8 0.1 fusion.26
  64.9 1.3 %collective-permute-start.5 = (f32[16,32,1]{2,1,0:T(8,128)S(1)}, f32[16,32,1]{2,1,0:T(8,128)S(1)}, u32[]{:S(2)}, u32[]{:S(2)}) collective-permute-start(f32[16,32,1]{2,1,0:T(8,128)S(1)} %get-tuple-element.23), channel_id=1, source_target_pairs={{8,0},{16,8},{24,16},{9,1},{17,9},{25,17},{10,2},{18,10},{26,18},{... | collective-permute-start | bytes 6152 | tf_op jit(solution)/shard_map/ppermute | solution.py:19
  66.2 3.0 %collective-permute-start.4 = (f32[16,32,1]{2,1,0:T(8,128)S(1)}, f32[16,32,1]{2,1,0:T(8,128)S(1)}, u32[]{:S(2)}, u32[]{:S(2)}) collective-permute-start(f32[16,32,1]{2,1,0:T(8,128)S(1)} %get-tuple-element.24), channel_id=1, source_target_pairs={{0,8},{8,16},{16,24},{1,9},{9,17},{17,25},{2,10},{10,18},{18,26},{... | collective-permute-start | bytes 6152 | tf_op jit(solution)/shard_map/ppermute | solution.py:18
  69.3 0.0 collective-permute-done.5
  69.3 1.1 %collective-permute-done.4 = f32[16,32,1]{2,1,0:T(8,128)S(1)} collective-permute-done((f32[16,32,1]{2,1,0:T(8,128)S(1)}, f32[16,32,1]{2,1,0:T(8,128)S(1)}, u32[]{:S(2)}, u32[]{:S(2)}) %collective-permute-start.4) | collective-permute-done | bytes 2080 | tf_op jit(solution)/shard_map/ppermute | solution.py:18
  70.4 0.2 pad_maximum_fusion.18
  70.6 1.3 %collective-permute-start.6 = (f32[16,1,130]{2,1,0:T(1,128)S(1)}, f32[16,1,130]{2,1,0:T(1,128)S(1)}, u32[]{:S(2)}, u32[]{:S(2)}) collective-permute-start(f32[16,1,130]{2,1,0:T(1,128)S(1)} %get-tuple-element.17), channel_id=1, source_target_pairs={{1,0},{2,1},{3,2},{4,3},{5,4},{6,5},{7,6},{9,8},{10,9},{11,10},{12... | collective-permute-start | bytes 24968 | tf_op jit(solution)/shard_map/ppermute | solution.py:19
  71.9 4.5 %collective-permute-start.7 = (f32[16,1,130]{2,1,0:T(1,128)S(1)}, f32[16,1,130]{2,1,0:T(1,128)S(1)}, u32[]{:S(2)}, u32[]{:S(2)}) collective-permute-start(f32[16,1,130]{2,1,0:T(1,128)S(1)} %get-tuple-element.18), channel_id=1, source_target_pairs={{0,1},{1,2},{2,3},{3,4},{4,5},{5,6},{6,7},{8,9},{9,10},{10,11},{11... | collective-permute-start | bytes 24968 | tf_op jit(solution)/shard_map/ppermute | solution.py:18
  76.5 0.0 collective-permute-done.6
  76.5 1.4 %collective-permute-done.7 = f32[16,1,130]{2,1,0:T(1,128)S(1)} collective-permute-done((f32[16,1,130]{2,1,0:T(1,128)S(1)}, f32[16,1,130]{2,1,0:T(1,128)S(1)}, u32[]{:S(2)}, u32[]{:S(2)}) %collective-permute-start.7) | collective-permute-done | bytes 8352 | tf_op jit(solution)/shard_map/ppermute | solution.py:18
  77.9 0.8 multiply_reduce_fusion
  78.6 19.4 %all-reduce = (f32[16]{0:T(128)S(1)}, f32[16]{0:T(128)S(1)}) all-reduce(f32[16]{0:T(128)S(1)} %get-tuple-element.3, f32[16]{0:T(128)S(1)} %get-tuple-element.2), channel_id=1, replica_groups=mesh['comp'=4,'dom'=8] {'dom'}, use_global_device_ids=true, to_apply=%region_9.10 | all-reduce | flops 32 | bytes 256 | tf_op jit(solution)/shard_map/psum | solution.py:38
  98.0 9.9 %all-reduce.2 = (f32[16]{0:T(128)S(1)}, f32[16]{0:T(128)S(1)}) all-reduce(f32[16]{0:T(128)S(1)} %get-tuple-element.6, f32[16]{0:T(128)S(1)} %get-tuple-element.7), channel_id=1, replica_groups=mesh['comp'=4,'dom'=8] {'comp'}, use_global_device_ids=true, to_apply=%region_10.11 | all-reduce | flops 32 | bytes 256 | tf_op jit(solution)/shard_map/psum | solution.py:38
  108.0 1.2 %multiply_subtract_fusion = (f32[16,32,128]{2,1,0:T(8,128)}, f32[16,32,128]{2,1,0:T(8,128)}) fusion(f32[16,32,128]{2,1,0:T(8,128)S(1)} %multiply_subtract_fusion.1, f32[16,32,128]{2,1,0:T(8,128)S(1)} %get-tuple-element.16, f32[16]{0:T(128)S(1)} %get-tuple-element.15, f32[16]{0:T(128)S(1)} %get-tuple-element.14, f32[16,32,1]{2,1,0:T(8,128)S(1)} %collective-permute-done.4, ...), kind=kLoop, calls=%fused_computation.28 | loop fusion | flops 1441792 | bytes 1348032 | tf_op jit(solution)/shard_map/sub | solution.py:84
  (11 shorter events, 0.1 us)
Async XLA Ops:
  0.6 8.1 %copy-start = (bf16[1,1,12,128,128]{4,3,2,1,0:T(8,128)(2,1)S(1)}, bf16[1,1,12,128,128]{4,3,2,1,0:T(8,128)(2,1)}, u32[]{:S(2)}) copy-start(bf16[1,1,12,128,128]{4,3,2,1,0:T(8,128)(2,1)} %param.8) | copy-start | bytes 1179652
  1.4 0.7 copy-start.2
  2.9 4.4 %copy-start.3 = (s32[1,1,12]{2,1,0:T(1,128)S(1)}, s32[1,1,12]{2,1,0:T(1,128)}, u32[]{:S(2)}) copy-start(s32[1,1,12]{2,1,0:T(1,128)} %param.6) | copy-start | bytes 148
  2.9 8.1 %all-to-all-start.1 = ((f32[4,4,1]{1,2,0:T(1,128)}), f32[4,4,1]{1,2,0:T(1,128)S(1)}, u32[]{:S(2)}, u32[]{:S(2)}) async-start(f32[4,4,1]{1,2,0:T(1,128)} %bitcast.8), calls=%async_computation.1 | async-start | bytes 4096 | tf_op jit(solution)/shard_map/all_to_all | solution.py:69
  11.0 7.9 %all-to-all-start = ((f32[16,16,128]{2,1,0:T(8,128)}), f32[16,16,128]{2,1,0:T(8,128)S(1)}, u32[]{:S(2)}, u32[]{:S(2)}) async-start(f32[16,16,128]{2,1,0:T(8,128)} %copy.11), calls=%async_computation | async-start | bytes 262144 | tf_op jit(solution)/shard_map/all_to_all | solution.py:68
  19.4 4.4 %collective-permute-start.1 = (f32[16,32,1]{2,1,0:T(8,128)S(1)}, f32[16,32,1]{2,1,0:T(8,128)S(1)}, u32[]{:S(2)}, u32[]{:S(2)}) collective-permute-start(f32[16,32,1]{2,1,0:T(8,128)S(1)} %get-tuple-element.25), channel_id=1, source_target_pairs={{8,0},{16,8},{24,16},{9,1},{17,9},{25,17},{10,2},{18,10},{26,18},{... | collective-permute-start | bytes 6152 | tf_op jit(solution)/shard_map/ppermute | solution.py:19
  20.7 10.2 %copy-start.1 = (f32[32,128]{1,0:T(8,128)S(1)}, f32[32,128]{1,0:T(8,128)}, u32[]{:S(2)}) copy-start(f32[32,128]{1,0:T(8,128)} %param.9) | copy-start | bytes 49156
  20.7 4.2 %collective-permute-start = (f32[16,32,1]{2,1,0:T(8,128)S(1)}, f32[16,32,1]{2,1,0:T(8,128)S(1)}, u32[]{:S(2)}, u32[]{:S(2)}) collective-permute-start(f32[16,32,1]{2,1,0:T(8,128)S(1)} %get-tuple-element.26), channel_id=1, source_target_pairs={{0,8},{8,16},{16,24},{1,9},{9,17},{17,25},{2,10},{10,18},{18,26},{... | collective-permute-start | bytes 6152 | tf_op jit(solution)/shard_map/ppermute | solution.py:18
  25.1 5.9 %collective-permute-start.2 = (f32[16,1,130]{2,1,0:T(1,128)S(1)}, f32[16,1,130]{2,1,0:T(1,128)S(1)}, u32[]{:S(2)}, u32[]{:S(2)}) collective-permute-start(f32[16,1,130]{2,1,0:T(1,128)S(1)} %get-tuple-element.19), channel_id=1, source_target_pairs={{1,0},{2,1},{3,2},{4,3},{5,4},{6,5},{7,6},{9,8},{10,9},{11,10},{12... | collective-permute-start | bytes 24968 | tf_op jit(solution)/shard_map/ppermute | solution.py:19
  26.4 6.0 %collective-permute-start.3 = (f32[16,1,130]{2,1,0:T(1,128)S(1)}, f32[16,1,130]{2,1,0:T(1,128)S(1)}, u32[]{:S(2)}, u32[]{:S(2)}) collective-permute-start(f32[16,1,130]{2,1,0:T(1,128)S(1)} %get-tuple-element.20), channel_id=1, source_target_pairs={{0,1},{1,2},{2,3},{3,4},{4,5},{5,6},{6,7},{8,9},{9,10},{10,11},{11... | collective-permute-start | bytes 24968 | tf_op jit(solution)/shard_map/ppermute | solution.py:18
  64.9 4.4 %collective-permute-start.5 = (f32[16,32,1]{2,1,0:T(8,128)S(1)}, f32[16,32,1]{2,1,0:T(8,128)S(1)}, u32[]{:S(2)}, u32[]{:S(2)}) collective-permute-start(f32[16,32,1]{2,1,0:T(8,128)S(1)} %get-tuple-element.23), channel_id=1, source_target_pairs={{8,0},{16,8},{24,16},{9,1},{17,9},{25,17},{10,2},{18,10},{26,18},{... | collective-permute-start | bytes 6152 | tf_op jit(solution)/shard_map/ppermute | solution.py:19
  66.2 4.2 %collective-permute-start.4 = (f32[16,32,1]{2,1,0:T(8,128)S(1)}, f32[16,32,1]{2,1,0:T(8,128)S(1)}, u32[]{:S(2)}, u32[]{:S(2)}) collective-permute-start(f32[16,32,1]{2,1,0:T(8,128)S(1)} %get-tuple-element.24), channel_id=1, source_target_pairs={{0,8},{8,16},{16,24},{1,9},{9,17},{17,25},{2,10},{10,18},{18,26},{... | collective-permute-start | bytes 6152 | tf_op jit(solution)/shard_map/ppermute | solution.py:18
  70.6 5.9 %collective-permute-start.6 = (f32[16,1,130]{2,1,0:T(1,128)S(1)}, f32[16,1,130]{2,1,0:T(1,128)S(1)}, u32[]{:S(2)}, u32[]{:S(2)}) collective-permute-start(f32[16,1,130]{2,1,0:T(1,128)S(1)} %get-tuple-element.17), channel_id=1, source_target_pairs={{1,0},{2,1},{3,2},{4,3},{5,4},{6,5},{7,6},{9,8},{10,9},{11,10},{12... | collective-permute-start | bytes 24968 | tf_op jit(solution)/shard_map/ppermute | solution.py:19
  71.9 6.0 %collective-permute-start.7 = (f32[16,1,130]{2,1,0:T(1,128)S(1)}, f32[16,1,130]{2,1,0:T(1,128)S(1)}, u32[]{:S(2)}, u32[]{:S(2)}) collective-permute-start(f32[16,1,130]{2,1,0:T(1,128)S(1)} %get-tuple-element.18), channel_id=1, source_target_pairs={{0,1},{1,2},{2,3},{3,4},{4,5},{5,6},{6,7},{8,9},{9,10},{10,11},{11... | collective-permute-start | bytes 24968 | tf_op jit(solution)/shard_map/ppermute | solution.py:18
